TPU v7x, 128 devices: a whole 4x4x4 slice. The times are simulated.
128 devices in a mesh: sample: 8 (over x, core), gene: 4 (over y), cohort: 4 (over z).
Axes of the slice: x: 4, y: 4, z: 4, core: 2. Of those that a mesh axis runs over, the one named last changes fastest.
Arguments:
- dosage: bfloat16 [16384, 32768], P(('sample', 'cohort'), 'gene'), may hold values from 0 to 2
- covariates: bfloat16 [16384, 32], P(('sample', 'cohort')), may hold values from 0 to 2
- phenotype: bfloat16 [16384], P(('sample', 'cohort')), may hold values from -6 to 6
- sample_mask: int32 [16384], P(('sample', 'cohort')), may hold values 0 or 1
- variant_weight: float32 [32768], replicated, may hold values from 0.1 to 1
- bucket_owner: int32 [256], replicated, may hold values from 0 to 15, as said below
- variant_gene: int32 [32768], replicated, may hold values from -1 to 127, as said below
Outputs:
- gram_tiles: float32 [16, 16, 128, 128], P(('gene', 'cohort'), 'sample')
- rho_stats: float32 [8, 128], P(None, ('gene', 'cohort'))
- gene_trace: float32 [128], P(('gene', 'cohort'))
Inputs may be any that keep to these rules, and one draw needn't show every extreme that they name: `bucket_owner`: every owner holds exactly 16 buckets, at most 8 of them among the 64 buckets of one index of gene, and some owner exactly 8; of the buckets of one index of gene, exactly 16 belong to owners whose index leaves a given remainder on division by the size of the cohort axis. `variant_gene`: genes o * 8 to (o + 1) * 8 - 1 lie in the buckets of owner o, each in one or more whole buckets that are consecutive among that owner's buckets; all its buckets are full but its last, whose first 10 to 128 columns are live and the rest -1.
All inputs are finite; a program needn't handle non-finite values. No bound on the sum of `sample_mask` on one device may be relied on, other than what follows from the above.
Results may differ from a plain program's by a relative error of at most 0.0003.
Values may be sent and summed in bfloat16 or wider, within the bound.
No kernel may reach another device: no remote copies, remote signals or barrier semaphores. Data moves between devices by JAX's collectives and lax.ppermute only.
A program may use at most 128 MiB of HBM per device.

v0:
```python
import math
import jax
import jax.numpy as jnp
from jax import lax
from jax.sharding import PartitionSpec as P

BUCKET_WIDTH = 128
GENES_OWN = 8
RHO_GRID = (0.0, 0.01, 0.04, 0.09, 0.16, 0.25, 0.5, 1.0)


def solve_moments(factor, rhs):
    half = lax.linalg.triangular_solve(factor, rhs, left_side=True, lower=True)
    return lax.linalg.triangular_solve(factor, half, left_side=True, lower=True, transpose_a=True)


def inner_rows(first, second):
    return lax.dot_general(
        first, second, (((0,), (0,)), ((), ())), preferred_element_type=jnp.float32
    )


def block_rank(labels, group_count, label_count):
    onehot = (labels[:, None] == jnp.arange(label_count, dtype=jnp.int32)[None, :]).astype(
        jnp.int32
    )
    blocks = onehot.reshape(group_count, labels.shape[0] // group_count, label_count)
    return jnp.sum((jnp.cumsum(blocks, axis=1) - blocks) * blocks, axis=2).reshape(labels.shape[0])


def finish_slots(
    gram, cross, slot_bucket, moments, variant_weight, variant_gene, owner_here, sample_total
):
    cov_count = moments.shape[0]
    slot_count = gram.shape[0]
    span_width = gram.shape[1]
    factor = jnp.linalg.cholesky(moments[:, :cov_count])
    beta_hat = solve_moments(factor, moments[:, cov_count:])[:, 0]
    cov_cross = cross[:, :cov_count, :]
    raw_score = cross[:, cov_count, :]
    stacked = jnp.transpose(cov_cross, (1, 0, 2)).reshape(cov_count, slot_count * span_width)
    solved = solve_moments(factor, stacked).reshape(cov_count, slot_count, span_width)
    projected = jnp.einsum("bcj,cbk->bjk", cov_cross, solved, precision=lax.Precision.HIGHEST)
    scores = raw_score - jnp.einsum(
        "bcj,c->bj", cov_cross, beta_hat, precision=lax.Precision.HIGHEST
    )
    bucket_total = variant_gene.shape[0] // span_width
    weight_rows = jnp.where(variant_gene >= 0, variant_weight, 0.0).reshape(
        bucket_total, span_width
    )
    live_weight = jnp.take(weight_rows, slot_bucket, axis=0)
    tiles = live_weight[:, :, None] * live_weight[:, None, :] * (gram - projected) / sample_total
    zscore = (live_weight * scores / math.sqrt(sample_total)).reshape(slot_count * span_width)
    gene_rows = (
        jnp.take(variant_gene.reshape(bucket_total, span_width), slot_bucket, axis=0)
        - owner_here * GENES_OWN
    )
    member = (
        gene_rows.reshape(slot_count * span_width)[:, None]
        == jnp.arange(GENES_OWN, dtype=jnp.int32)[None, :]
    ).astype(jnp.float32)
    squares = jnp.dot(zscore * zscore, member, precision=lax.Precision.HIGHEST)
    burden_sum = jnp.dot(zscore, member, precision=lax.Precision.HIGHEST)
    diagonal = jnp.diagonal(tiles, axis1=1, axis2=2).reshape(slot_count * span_width)
    trace_sum = jnp.dot(diagonal, member, precision=lax.Precision.HIGHEST)
    return (tiles, squares, burden_sum, trace_sum)


def shards(dosage, covariates, phenotype, sample_mask, variant_weight, bucket_owner, variant_gene):
    gene_count = lax.axis_size("gene")
    cohort_count = lax.axis_size("cohort")
    sample_count = lax.axis_size("sample")
    owner_count = gene_count * cohort_count
    span_width = BUCKET_WIDTH
    sample_rows = dosage.shape[0]
    src_buckets = dosage.shape[1] // span_width
    total_buckets = bucket_owner.shape[0]
    held_slots = total_buckets // owner_count
    cap_slots = held_slots // 2
    share = held_slots // sample_count
    sample_total = sample_rows * sample_count * cohort_count
    cohort_here = lax.axis_index("cohort")
    owner_here = lax.axis_index("gene") * cohort_count + cohort_here
    sample_keep = sample_mask.astype(jnp.bfloat16)
    masked_cov = covariates * sample_keep[:, None]
    left_cols = jnp.concatenate([masked_cov, (phenotype * sample_keep)[:, None]], axis=1)
    moments = lax.psum(
        inner_rows(masked_cov, jnp.concatenate([covariates, phenotype[:, None]], axis=1)),
        ("sample", "cohort"),
    )
    masked_dosage = (dosage * sample_keep[:, None]).reshape(sample_rows, src_buckets, span_width)
    owner_ids = jnp.arange(owner_count, dtype=jnp.int32)
    onehot = (bucket_owner[:, None] == owner_ids[None, :]).astype(jnp.int32)
    owner_rank = jnp.sum((jnp.cumsum(onehot, axis=0) - onehot) * onehot, axis=1)
    pair_rank = block_rank(bucket_owner, gene_count, owner_count)
    source_start = lax.axis_index("gene") * src_buckets
    mine_owner = lax.dynamic_slice_in_dim(bucket_owner, source_start, src_buckets)
    mine_rank = lax.dynamic_slice_in_dim(pair_rank, source_start, src_buckets)
    own_key = jnp.where(bucket_owner == owner_here, owner_rank, held_slots)
    own_bucket = (
        jnp.zeros((held_slots,), jnp.int32)
        .at[own_key]
        .set(jnp.arange(total_buckets, dtype=jnp.int32), mode="drop")
    )
    own_source = own_bucket // src_buckets
    own_pair = jnp.take(pair_rank, own_bucket)
    cohort_ids = jnp.arange(cohort_count, dtype=jnp.int32)
    flat_index = (
        (own_source[None, :] * cohort_count + cohort_ids[:, None]) * cap_slots + own_pair[None, :]
    ).reshape(cohort_count * held_slots)
    send_from = (
        jnp.full((owner_count * cap_slots,), -1, jnp.int32)
        .at[mine_owner * cap_slots + mine_rank]
        .set(jnp.arange(src_buckets, dtype=jnp.int32))
    )
    send_pick = jnp.maximum(send_from, 0)
    cohort_left = lax.all_gather(left_cols[:, None, :], "cohort", axis=1, tiled=True)
    packed = (
        jnp.take(masked_dosage, send_pick, axis=1)
        * (send_from >= 0).astype(jnp.bfloat16)[None, :, None]
    )
    packed = packed.reshape(sample_rows, owner_count, cap_slots, span_width)
    arrived = lax.all_to_all(packed, ("gene", "cohort"), split_axis=1, concat_axis=1, tiled=True)
    arrived = arrived.reshape(sample_rows, owner_count * cap_slots, span_width)
    owned = jnp.take(arrived, flat_index, axis=1).reshape(
        sample_rows, cohort_count, held_slots, span_width
    )
    gram = jnp.einsum("schj,schk->hjk", owned, owned, preferred_element_type=jnp.float32)
    cross = jnp.einsum("sci,schk->hik", cohort_left, owned, preferred_element_type=jnp.float32)
    slot_start = lax.axis_index("sample") * share
    gram, cross = lax.psum((gram, cross), "sample")
    tiles, squares, burden_sum, trace_sum = finish_slots(
        gram, cross, own_bucket, moments, variant_weight, variant_gene, owner_here, sample_total
    )
    tiles = lax.dynamic_slice_in_dim(tiles, slot_start, share)
    rho_col = jnp.array(RHO_GRID, dtype=jnp.float32)[:, None]
    rho_stats = (
        (1.0 - rho_col) * squares[None, :] + rho_col * (burden_sum * burden_sum)[None, :]
    ) / span_width
    gene_trace = trace_sum / span_width
    return (tiles[None], rho_stats, gene_trace)


def solution(mesh):
    placed = (
        P(("sample", "cohort"), "gene"),
        P(("sample", "cohort"), None),
        P(("sample", "cohort")),
        P(("sample", "cohort")),
        P(),
        P(),
        P(),
    )
    return jax.shard_map(
        shards,
        mesh=mesh,
        in_specs=placed,
        out_specs=(
            P(("gene", "cohort"), "sample", None, None),
            P(None, ("gene", "cohort")),
            P(("gene", "cohort")),
        ),
        check_vma=False,
    )
```

profile of v0, /device:TPU:0, one launch (start us, length us, event | category | flops | bytes accessed | tf_op | source)
XLA Modules:
  0.0 636.7 jit_solution(13550545437215399836)
XLA Ops:
  10.1 12.0 %copy.54 = bf16[512,8192]{0,1:T(8,128)(2,1)} copy(bf16[512,8192]{1,0:T(8,128)(2,1)} %param.8) | data formatting | bytes 16777216 | tf_op args[0]
  22.1 7.1 %broadcast_multiply_fusion = bf16[512,8192]{0,1:T(8,128)(2,1)} fusion(bf16[512,8192]{0,1:T(8,128)(2,1)} %copy.54, bf16[512]{0:T(512)(128)(2,1)S(1)} %get-tuple-element.9), kind=kLoop, calls=%fused_computation.14 | loop fusion | flops 4194304 | bytes 16778240 | tf_op jit(solution)/shard_map/mul | solution.py:91
  29.2 11.9 %copy.55 = bf16[512,64,128]{2,0,1:T(8,128)(2,1)} copy(bf16[512,64,128]{0,2,1:T(8,128)(2,1)} %bitcast.130) | data formatting | bytes 16777216 | tf_op jit(solution)/shard_map/reshape | solution.py:91
  41.3 11.5 %gather_fusion.2 = bf16[128,512,128]{2,1,0:T(8,128)(2,1)} fusion(bf16[512,64,128]{2,0,1:T(8,128)(2,1)} %copy.55, s32[1024]{0:T(1024)S(1)} %pad_clamp_fusion.1), kind=kCustom, calls=%fused_computation.2 | custom fusion | bytes 33554944 | tf_op jit(solution)/shard_map/jit(_take)/gather | solution.py:119
  52.8 14.2 %select_multiply_fusion = bf16[512,16,8,128]{3,0,2,1:T(8,128)(2,1)} fusion(bf16[512,16,8,128]{3,0,2,1:T(8,128)(2,1)} %bitcast.127, pred[16,8]{1,0:T(8,128)(4,1)S(1)} %broadcast_in_dim.106, bf16[16,8]{1,0:T(8,128)(2,1)S(1)} %reshape.226), kind=kLoop, calls=%fused_computation.8 | loop fusion | flops 16777216 | bytes 33554816 | tf_op jit(solution)/shard_map/mul | solution.py:119
  67.0 8.3 %all-to-all-start = ((bf16[512,16,8,128]{3,0,2,1:T(8,128)(2,1)}), bf16[512,16,8,128]{3,0,2,1:T(8,128)(2,1)}, u32[]{:S(2)}, u32[]{:S(2)}) async-start(bf16[512,16,8,128]{3,0,2,1:T(8,128)(2,1)} %select_multiply_fusion), calls=%async_computation | async-start | bytes 33554432 | tf_op jit(solution)/shard_map/all_to_all | solution.py:123
  76.4 1.4 scatter_custom_fusion
  78.6 160.0 %all-gather.1 = bf16[4,33,512]{2,1,0:T(8,128)(2,1)S(1)} all-gather(bf16[1,33,512]{2,1,0:T(8,128)(2,1)S(1)} %maximum_bitcast_fusion), channel_id=2, replica_groups=mesh['sample'=8,'gene'=4,'cohort'=4] {'cohort'}, dimensions={0}, use_global_device_ids=true | all-gather | bytes 168960 | tf_op jit(solution)/shard_map/all_gather | solution.py:117
  238.9 197.3 %psum.23 = f32[32,33]{0,1:T(8,128)S(1)} all-reduce(f32[32,33]{0,1:T(8,128)S(1)} %fusion.24), channel_id=1, replica_groups=mesh['sample'=8,'gene'=4,'cohort'=4] {'sample','cohort'}, use_global_device_ids=true, to_apply=%region_9.10 | all-reduce | flops 1056 | bytes 8448 | tf_op jit(solution)/shard_map/psum | solution.py:87
  436.3 2.9 cholesky.16
  440.5 2.4 custom-call.12
  444.2 11.7 %gather_fusion.3 = bf16[64,512,128]{2,1,0:T(8,128)(2,1)} fusion(bf16[512,128,128]{2,0,1:T(8,128)(2,1)} %bitcast.6, s32[1024]{0:T(1024)S(1)} %pad_clamp_fusion), kind=kCustom, calls=%fused_computation.3 | custom fusion | bytes 16777472 | tf_op jit(solution)/shard_map/jit(_take)/gather | solution.py:125
  456.0 12.0 %copy.56 = bf16[512,64,128]{2,1,0:T(8,128)(2,1)} copy(bf16[512,64,128]{2,0,1:T(8,128)(2,1)} %bitcast.128) | data formatting | bytes 16777216 | tf_op jit(solution)/shard_map/jit(_take)/gather | solution.py:125
  467.9 7.4 %broadcast_select_fusion = bf16[512,4,16,128]{3,2,1,0:T(8,128)(2,1)} fusion(bf16[512,4,16,128]{3,2,1,0:T(8,128)(2,1)} %bitcast.129, pred[4,16]{1,0:T(4,128)(4,1)S(1)} %compare_and_fusion), kind=kLoop, calls=%fused_computation.9 | loop fusion | flops 4194304 | bytes 16777280 | tf_op jit(solution)/shard_map/jit(_take)/select_n | solution.py:125
  475.3 25.9 %fusion.4 = f32[16,128,128]{2,1,0:T(8,128)} fusion(bf16[512,4,16,128]{3,2,1,0:T(8,128)(2,1)} %broadcast_select_fusion), kind=kOutput, calls=%fused_computation.15 | convolution fusion | flops 1073741824 | bytes 9437184 | tf_op jit(solution)/shard_map/schj,schk->hjk/dot_general | solution.py:128
  501.2 8.8 %fusion.9 = f32[16,33,128]{2,1,0:T(8,128)} fusion(bf16[512,4,33,1]{0,2,1,3:T(8,128)(2,1)S(1)} %reshape.299, bf16[512,4,16,128]{3,2,1,0:T(8,128)(2,1)} %broadcast_select_fusion), kind=kOutput, calls=%fused_computation.19 | convolution fusion | flops 276824064 | bytes 8794112 | tf_op jit(solution)/shard_map/sci,schk->hik/dot_general | solution.py:129
  510.4 101.9 %all-reduce.3.cloned.1.call-done = (f32[16,128,128]{2,1,0:T(8,128)}, f32[16,33,128]{2,1,0:T(8,128)}) async-done(((f32[16,128,128]{2,1,0:T(8,128)}, f32[16,33,128]{2,1,0:T(8,128)}), (f32[16,128,128]{2,1,0:T(8,128)}, f32[16,33,128]{2,1,0:T(8,128)})) %all-reduce.3.cloned.1.call-update) | async-done | bytes 1318928 | tf_op jit(solution)/shard_map/psum | solution.py:131
  612.3 0.8 slice.59
  613.1 1.4 fusion.17
  614.5 1.2 fusion.20
  616.2 3.3 fusion.8
  619.5 4.6 copy.65
  624.1 1.8 gather_fusion.5
  626.0 1.1 fusion.12
  (77 shorter events, 11.0 us)
Async XLA Ops:
  10.1 12.0 %copy-start.4 = (bf16[512]{0:T(512)(128)(2,1)S(1)}, bf16[512]{0:T(512)(128)(2,1)}, u32[]{:S(2)}) copy-start(bf16[512]{0:T(512)(128)(2,1)} %param.10) | copy-start | bytes 3076
  10.1 12.0 %copy-start.5 = (s32[512]{0:T(512)S(1)}, s32[512]{0:T(512)}, u32[]{:S(2)}) copy-start(s32[512]{0:T(512)} %param.11) | copy-start | bytes 6148
  67.0 8.4 %copy-start.3 = (s32[256]{0:T(256)S(1)}, s32[256]{0:T(256)}, u32[]{:S(2)}) copy-start(s32[256]{0:T(256)} %param.13) | copy-start | bytes 3076
  67.0 11.6 %copy-start.2 = (bf16[512,32]{0,1:T(8,128)(2,1)S(1)}, bf16[512,32]{0,1:T(8,128)(2,1)}, u32[]{:S(2)}) copy-start(bf16[512,32]{0,1:T(8,128)(2,1)} %param.9) | copy-start | bytes 98308
  67.0 375.9 %copy-start = (s32[32768]{0:T(1024)S(1)}, s32[32768]{0:T(1024)}, u32[]{:S(2)}) copy-start(s32[32768]{0:T(1024)} %param.14) | copy-start | bytes 393220
  67.0 375.9 %copy-start.1 = (f32[32768]{0:T(1024)S(1)}, f32[32768]{0:T(1024)}, u32[]{:S(2)}) copy-start(f32[32768]{0:T(1024)} %param.12) | copy-start | bytes 393220
  67.0 377.2 %all-to-all-start = ((bf16[512,16,8,128]{3,0,2,1:T(8,128)(2,1)}), bf16[512,16,8,128]{3,0,2,1:T(8,128)(2,1)}, u32[]{:S(2)}, u32[]{:S(2)}) async-start(bf16[512,16,8,128]{3,0,2,1:T(8,128)(2,1)} %select_multiply_fusion), calls=%async_computation | async-start | bytes 33554432 | tf_op jit(solution)/shard_map/all_to_all | solution.py:123
  75.4 536.9 %all-reduce.3.cloned.1.call-start = ((), (), s32[]{:S(2)}) async-start(), calls=%async_computation.1 | async-start | bytes 2752512 | tf_op jit(solution)/shard_map/psum | solution.py:131
  510.0 119.0 %copy-start.6 = (f32[8]{0:T(128)S(1)}, f32[8]{0:T(128)}, u32[]{:S(2)}) copy-start(f32[8]{0:T(128)} %constant.200.clone) | copy-start | bytes 100
  510.0 119.0 %copy-start.7 = (f32[8]{0:T(128)S(1)}, f32[8]{0:T(128)}, u32[]{:S(2)}) copy-start(f32[8]{0:T(128)} %constant.202) | copy-start | bytes 100
Sparse Core Ops, SparseCore 0:
  510.1 102.1 all-reduce.2
where the time goes:
time: 643 us; the launch traced here: 637 us
  blocking collectives  357 us (56%)
  waiting for transfers between devices  102 us (16%)
  local copies, waits for them, and re-layouts  72.6 us (11%)
  matrix products  43.6 us (7%)
  other arithmetic  38.3 us (6%)
  between operations  14.6 us (2%)
  starting transfers between devices  8.38 us (1%)
    psum x1, blocking collectives, shards(): lax.psum(inner_rows(masked_cov, jnp.concatenate([covariates, phenotype[:,...  197 us
    all_gather x1, blocking collectives, shards(): lax.all_gather(left_cols[:, None, :], 'cohort', axis=1, tiled=True)  160 us
    psum x1, waiting for transfers between devices, shards(): gram, cross = lax.psum((gram, cross), 'sample')  102 us
    dot_general x1, matrix products, shards(): jnp.einsum('schj,schk->hjk', owned, owned, preferred_element_type=jnp.flo...  25.9 us
    gather x2, local copies, waits for them, and re-layouts, shards(): jnp.take(arrived, flat_index, axis=1)  23.7 us
    mul x2, other arithmetic, shards(): jnp.take(masked_dosage, send_pick, axis=1)  14.2 us
  transfers between devices with their start and end apart: 2, of which 1 were waited for; matrix products, arithmetic and copies ran while one was open for 2% of the time, Pallas kernels for 0%

commit v1 on v0

--- a/solution.py
+++ b/solution.py
@@ -85,8 +85,11 @@
     masked_cov = covariates * sample_keep[:, None]
     left_cols = jnp.concatenate([masked_cov, (phenotype * sample_keep)[:, None]], axis=1)
     moments = lax.psum(
-        inner_rows(masked_cov, jnp.concatenate([covariates, phenotype[:, None]], axis=1)),
-        ("sample", "cohort"),
+        lax.psum(
+            inner_rows(masked_cov, jnp.concatenate([covariates, phenotype[:, None]], axis=1)),
+            "sample",
+        ),
+        "cohort",
     )
     masked_dosage = (dosage * sample_keep[:, None]).reshape(sample_rows, src_buckets, span_width)
     owner_ids = jnp.arange(owner_count, dtype=jnp.int32)

time: 643 us -> 546 us (0.85)
  blocking collectives: 357 us -> 271 us
  waiting for transfers between devices: 102 us -> 90.3 us
    psum x1, blocking collectives: 197 us -> 27.3 us  [shards(): lax.psum(inner_rows(masked_cov, jnp.concatenate([covariates, phenotype[:,...]
    psum x0 -> x1, blocking collectives: none -> 83.5 us  [shards(): lax.psum(lax.psum(inner_rows(masked_cov, jnp.concatenate([covariates, phe...]
    psum x1, waiting for transfers between devices: 102 us -> 79.2 us  [shards(): gram, cross = lax.psum((gram, cross), 'sample')]
    all_to_all x1, waiting for transfers between devices: 0.01 us -> 11.1 us  [shards(): lax.all_to_all(packed, ('gene', 'cohort'), split_axis=1, concat_axis=1, t...]
  transfers between devices with their start and end apart: 2 -> 2, of which waited for: 1 -> 2; matrix products, arithmetic and copies ran while one was open for 2% -> 2% of each run, Pallas kernels for 0% -> 0%
where the time goes in v1:
time: 546 us; the launch traced here: 539 us
  blocking collectives  271 us (50%)
  waiting for transfers between devices  90.3 us (17%)
  local copies, waits for them, and re-layouts  72.6 us (13%)
  matrix products  43.6 us (8%)
  other arithmetic  38.3 us (7%)
  between operations  14.6 us (3%)
  starting transfers between devices  8.38 us (2%)
    all_gather x1, blocking collectives, shards(): lax.all_gather(left_cols[:, None, :], 'cohort', axis=1, tiled=True)  160 us
    psum x1, blocking collectives, shards(): lax.psum(lax.psum(inner_rows(masked_cov, jnp.concatenate([covariates, phe...  83.5 us
    psum x1, waiting for transfers between devices, shards(): gram, cross = lax.psum((gram, cross), 'sample')  79.2 us
    psum x1, blocking collectives, shards(): lax.psum(inner_rows(masked_cov, jnp.concatenate([covariates, phenotype[:,...  27.3 us
    dot_general x1, matrix products, shards(): jnp.einsum('schj,schk->hjk', owned, owned, preferred_element_type=jnp.flo...  25.9 us
    gather x2, local copies, waits for them, and re-layouts, shards(): jnp.take(arrived, flat_index, axis=1)  23.7 us
    mul x2, other arithmetic, shards(): jnp.take(masked_dosage, send_pick, axis=1)  14.2 us
    unnamed x18, local copies, waits for them, and re-layouts  12 us
  transfers between devices with their start and end apart: 2, of which 2 were waited for; matrix products, arithmetic and copies ran while one was open for 2% of the time, Pallas kernels for 0%

profile of v1, /device:TPU:0, one launch (start us, length us, event | category | flops | bytes accessed | tf_op | source)
XLA Modules:
  0.0 538.6 jit_solution(18349729008207832718)
XLA Ops:
  10.1 12.0 %copy.54 = bf16[512,8192]{0,1:T(8,128)(2,1)} copy(bf16[512,8192]{1,0:T(8,128)(2,1)} %param.8) | data formatting | bytes 16777216 | tf_op args[0]
  22.1 7.1 %broadcast_multiply_fusion = bf16[512,8192]{0,1:T(8,128)(2,1)} fusion(bf16[512,8192]{0,1:T(8,128)(2,1)} %copy.54, bf16[512]{0:T(512)(128)(2,1)S(1)} %get-tuple-element.9), kind=kLoop, calls=%fused_computation.14 | loop fusion | flops 4194304 | bytes 16778240 | tf_op jit(solution)/shard_map/mul | solution.py:94
  29.2 11.9 %copy.55 = bf16[512,64,128]{2,0,1:T(8,128)(2,1)} copy(bf16[512,64,128]{0,2,1:T(8,128)(2,1)} %bitcast.130) | data formatting | bytes 16777216 | tf_op jit(solution)/shard_map/reshape | solution.py:94
  41.3 11.5 %gather_fusion.2 = bf16[128,512,128]{2,1,0:T(8,128)(2,1)} fusion(bf16[512,64,128]{2,0,1:T(8,128)(2,1)} %copy.55, s32[1024]{0:T(1024)S(1)} %pad_clamp_fusion.1), kind=kCustom, calls=%fused_computation.2 | custom fusion | bytes 33554944 | tf_op jit(solution)/shard_map/jit(_take)/gather | solution.py:122
  52.8 14.2 %select_multiply_fusion = bf16[512,16,8,128]{3,0,2,1:T(8,128)(2,1)} fusion(bf16[512,16,8,128]{3,0,2,1:T(8,128)(2,1)} %bitcast.127, pred[16,8]{1,0:T(8,128)(4,1)S(1)} %broadcast_in_dim.106, bf16[16,8]{1,0:T(8,128)(2,1)S(1)} %reshape.226), kind=kLoop, calls=%fused_computation.8 | loop fusion | flops 16777216 | bytes 33554816 | tf_op jit(solution)/shard_map/mul | solution.py:122
  67.0 8.3 %all-to-all-start = ((bf16[512,16,8,128]{3,0,2,1:T(8,128)(2,1)}), bf16[512,16,8,128]{3,0,2,1:T(8,128)(2,1)}, u32[]{:S(2)}, u32[]{:S(2)}) async-start(bf16[512,16,8,128]{3,0,2,1:T(8,128)(2,1)} %select_multiply_fusion), calls=%async_computation | async-start | bytes 33554432 | tf_op jit(solution)/shard_map/all_to_all | solution.py:126
  76.4 1.4 scatter_custom_fusion
  78.6 160.0 %all-gather.1 = bf16[4,33,512]{2,1,0:T(8,128)(2,1)S(1)} all-gather(bf16[1,33,512]{2,1,0:T(8,128)(2,1)S(1)} %maximum_bitcast_fusion), channel_id=2, replica_groups=mesh['sample'=8,'gene'=4,'cohort'=4] {'cohort'}, dimensions={0}, use_global_device_ids=true | all-gather | bytes 168960 | tf_op jit(solution)/shard_map/all_gather | solution.py:120
  238.9 27.3 %psum.30 = f32[32,33]{0,1:T(8,128)S(1)} all-reduce(f32[32,33]{0,1:T(8,128)S(1)} %fusion.24), channel_id=1, replica_groups=mesh['sample'=8,'gene'=4,'cohort'=4] {'sample'}, use_global_device_ids=true, to_apply=%region_9.10 | all-reduce | flops 1056 | bytes 8448 | tf_op jit(solution)/shard_map/psum | solution.py:88
  266.2 83.5 %psum.31 = f32[32,33]{0,1:T(8,128)S(1)} all-reduce(f32[32,33]{0,1:T(8,128)S(1)} %psum.30), channel_id=1, replica_groups=mesh['sample'=8,'gene'=4,'cohort'=4] {'cohort'}, use_global_device_ids=true, to_apply=%region_10.11 | all-reduce | flops 1056 | bytes 8448 | tf_op jit(solution)/shard_map/psum | solution.py:87
  349.8 2.9 cholesky.16
  354.1 2.4 custom-call.12
  357.7 11.1 %all-to-all-done = bf16[512,16,8,128]{3,0,2,1:T(8,128)(2,1)} async-done(((bf16[512,16,8,128]{3,0,2,1:T(8,128)(2,1)}), bf16[512,16,8,128]{3,0,2,1:T(8,128)(2,1)}, u32[]{:S(2)}, u32[]{:S(2)}) %all-to-all-start) | async-done | bytes 16777248 | tf_op jit(solution)/shard_map/all_to_all | solution.py:126
  368.9 11.7 %gather_fusion.3 = bf16[64,512,128]{2,1,0:T(8,128)(2,1)} fusion(bf16[512,128,128]{2,0,1:T(8,128)(2,1)} %bitcast.6, s32[1024]{0:T(1024)S(1)} %pad_clamp_fusion), kind=kCustom, calls=%fused_computation.3 | custom fusion | bytes 16777472 | tf_op jit(solution)/shard_map/jit(_take)/gather | solution.py:128
  380.6 12.0 %copy.56 = bf16[512,64,128]{2,1,0:T(8,128)(2,1)} copy(bf16[512,64,128]{2,0,1:T(8,128)(2,1)} %bitcast.128) | data formatting | bytes 16777216 | tf_op jit(solution)/shard_map/jit(_take)/gather | solution.py:128
  392.6 7.4 %broadcast_select_fusion = bf16[512,4,16,128]{3,2,1,0:T(8,128)(2,1)} fusion(bf16[512,4,16,128]{3,2,1,0:T(8,128)(2,1)} %bitcast.129, pred[4,16]{1,0:T(4,128)(4,1)S(1)} %compare_and_fusion), kind=kLoop, calls=%fused_computation.9 | loop fusion | flops 4194304 | bytes 16777280 | tf_op jit(solution)/shard_map/jit(_take)/select_n | solution.py:128
  400.0 25.9 %fusion.4 = f32[16,128,128]{2,1,0:T(8,128)} fusion(bf16[512,4,16,128]{3,2,1,0:T(8,128)(2,1)} %broadcast_select_fusion), kind=kOutput, calls=%fused_computation.15 | convolution fusion | flops 1073741824 | bytes 9437184 | tf_op jit(solution)/shard_map/schj,schk->hjk/dot_general | solution.py:131
  425.9 8.8 %fusion.9 = f32[16,33,128]{2,1,0:T(8,128)} fusion(bf16[512,4,33,1]{0,2,1,3:T(8,128)(2,1)S(1)} %reshape.299, bf16[512,4,16,128]{3,2,1,0:T(8,128)(2,1)} %broadcast_select_fusion), kind=kOutput, calls=%fused_computation.19 | convolution fusion | flops 276824064 | bytes 8794112 | tf_op jit(solution)/shard_map/sci,schk->hik/dot_general | solution.py:132
  435.0 79.2 %all-reduce.3.cloned.1.call-done = (f32[16,128,128]{2,1,0:T(8,128)}, f32[16,33,128]{2,1,0:T(8,128)}) async-done(((f32[16,128,128]{2,1,0:T(8,128)}, f32[16,33,128]{2,1,0:T(8,128)}), (f32[16,128,128]{2,1,0:T(8,128)}, f32[16,33,128]{2,1,0:T(8,128)})) %all-reduce.3.cloned.1.call-update) | async-done | bytes 1318928 | tf_op jit(solution)/shard_map/psum | solution.py:134
  515.1 1.4 fusion.17
  516.4 1.2 fusion.20
  518.1 3.3 fusion.8
  521.4 4.6 copy.65
  526.0 1.8 gather_fusion.5
  (78 shorter events, 13.0 us)
Async XLA Ops:
  10.1 12.0 %copy-start.4 = (bf16[512]{0:T(512)(128)(2,1)S(1)}, bf16[512]{0:T(512)(128)(2,1)}, u32[]{:S(2)}) copy-start(bf16[512]{0:T(512)(128)(2,1)} %param.10) | copy-start | bytes 3076
  10.1 12.0 %copy-start.5 = (s32[512]{0:T(512)S(1)}, s32[512]{0:T(512)}, u32[]{:S(2)}) copy-start(s32[512]{0:T(512)} %param.11) | copy-start | bytes 6148
  67.0 8.4 %copy-start.3 = (s32[256]{0:T(256)S(1)}, s32[256]{0:T(256)}, u32[]{:S(2)}) copy-start(s32[256]{0:T(256)} %param.13) | copy-start | bytes 3076
  67.0 11.6 %copy-start.2 = (bf16[512,32]{0,1:T(8,128)(2,1)S(1)}, bf16[512,32]{0,1:T(8,128)(2,1)}, u32[]{:S(2)}) copy-start(bf16[512,32]{0,1:T(8,128)(2,1)} %param.9) | copy-start | bytes 98308
  67.0 289.5 %copy-start = (s32[32768]{0:T(1024)S(1)}, s32[32768]{0:T(1024)}, u32[]{:S(2)}) copy-start(s32[32768]{0:T(1024)} %param.14) | copy-start | bytes 393220
  67.0 289.5 %copy-start.1 = (f32[32768]{0:T(1024)S(1)}, f32[32768]{0:T(1024)}, u32[]{:S(2)}) copy-start(f32[32768]{0:T(1024)} %param.12) | copy-start | bytes 393220
  67.0 301.8 %all-to-all-start = ((bf16[512,16,8,128]{3,0,2,1:T(8,128)(2,1)}), bf16[512,16,8,128]{3,0,2,1:T(8,128)(2,1)}, u32[]{:S(2)}, u32[]{:S(2)}) async-start(bf16[512,16,8,128]{3,0,2,1:T(8,128)(2,1)} %select_multiply_fusion), calls=%async_computation | async-start | bytes 33554432 | tf_op jit(solution)/shard_map/all_to_all | solution.py:126
  75.4 438.8 %all-reduce.3.cloned.1.call-start = ((), (), s32[]{:S(2)}) async-start(), calls=%async_computation.1 | async-start | bytes 2752512 | tf_op jit(solution)/shard_map/psum | solution.py:134
  434.7 96.2 %copy-start.6 = (f32[8]{0:T(128)S(1)}, f32[8]{0:T(128)}, u32[]{:S(2)}) copy-start(f32[8]{0:T(128)} %constant.200.clone) | copy-start | bytes 100
  434.7 96.2 %copy-start.7 = (f32[8]{0:T(128)S(1)}, f32[8]{0:T(128)}, u32[]{:S(2)}) copy-start(f32[8]{0:T(128)} %constant.202) | copy-start | bytes 100
Sparse Core Ops, SparseCore 0:
  434.8 79.3 all-reduce.2
